TPU v7x, 128 devices: a whole 4x4x4 slice. The times are simulated.
128 devices in a mesh: req: 32 (over x, z, core), head: 4 (over y).
Axes of the slice: x: 4, y: 4, z: 4, core: 2. Of those that a mesh axis runs over, the one named last changes fastest.
Arguments:
- streams: bfloat16 [128, 64, 4, 2048], P('req'), may hold values from -6 to 6
- w_query: bfloat16 [2048, 2048], P(None, 'head'), may hold values from -0.125 to 0.125
- w_key: bfloat16 [2048, 2048], P(None, 'head'), may hold values from -0.125 to 0.125
- w_value: bfloat16 [2048, 2048], P(None, 'head'), may hold values from -0.125 to 0.125
- w_output: bfloat16 [2048, 2048], P('head'), may hold values from -0.125 to 0.125
- w_gate: bfloat16 [2048, 8192], P(None, 'req'), may hold values from -0.125 to 0.125
- w_up: bfloat16 [2048, 8192], P(None, 'req'), may hold values from -0.125 to 0.125
- w_down: bfloat16 [8192, 2048], P('req'), may hold values from -0.0625 to 0.0625
- cache_keys: bfloat16 [128, 1024, 2048], P('req', None, 'head'), may hold values from -250 to 250
- cache_values: bfloat16 [128, 1024, 2048], P('req', None, 'head'), may hold values from -6 to 6
- hc_in: float32 [2, 4], replicated, may hold values from 0.1 to 0.6
- hc_res: float32 [2, 4, 4], replicated, may hold values from -0.4 to 0.8
- hc_out: float32 [2, 4], replicated, may hold values from 0.5 to 1.5
- parents: int32 [128, 64], replicated, may hold values from 0 to 62, as said below
- draft_len: int32 [128], replicated, may hold values from 1 to 64, 6144 in all
- cache_len: int32 [128], replicated, may hold values from 1 to 1024, 65536 in all
- accept_pick: int32 [128], replicated, may hold values from 0 to 63
- slot_owner: int32 [128], replicated, may hold values from 0 to 127, each once
Outputs:
- new_streams: bfloat16 [128, 64, 4, 2048], P('req', 'head')
- accepted_kv: bfloat16 [128, 64, 2, 2048], P('req', None, None, 'head')
Inputs may be any that keep to these rules, and one draw needn't show every extreme that they name: parents[r, 0] = 0 and 0 <= parents[r, p] < p for p >= 1. `draft_len`: the live draft nodes of all requests sum to exactly 6144.
All inputs are finite; a program needn't handle non-finite values.
Results may differ from a plain program's by a relative error of at most 0.024.
Values may be sent and summed in bfloat16 or wider, within the bound.
No kernel may reach another device: no remote copies, remote signals or barrier semaphores. Data moves between devices by JAX's collectives and lax.ppermute only.
A program may use at most 128 MiB of HBM per device.

v0:
```python
import jax
import jax.numpy as jnp
from jax import lax
from jax.sharding import PartitionSpec as P

HD = 128


def ancestry(parent_ids):
    count = parent_ids.shape[-1]
    nodes = jnp.arange(count, dtype=jnp.int32)
    links = (parent_ids[..., :, None] == nodes).astype(jnp.float32)
    unit = (nodes[:, None] == nodes[None, :]).astype(jnp.float32)
    above = jnp.minimum(links + unit, 1.0)
    for rounds in range((count - 1).bit_length()):
        above = jnp.minimum(jnp.matmul(above, above, precision=lax.Precision.HIGHEST), 1.0)
    depth = jnp.sum(above, axis=-1) - 1.0
    return (above, depth)


def normalize(values):
    center = jnp.mean(values, axis=-1, keepdims=True)
    spread = jnp.mean(jnp.square(values - center), axis=-1, keepdims=True)
    return (values - center) * lax.rsqrt(spread + 1e-05)


def rotate(values, position, head_size):
    half = head_size // 2
    freq = jnp.power(10000.0, -(jnp.arange(half, dtype=jnp.float32) * 2.0 / head_size))
    angle = position[..., None] * freq
    shaped = values.reshape(values.shape[:-1] + (-1, head_size))
    first, second = (shaped[..., :half], shaped[..., half:])
    cosine = jnp.cos(angle)[..., None, :]
    sine = jnp.sin(angle)[..., None, :]
    turned = jnp.concatenate(
        [first * cosine - second * sine, second * cosine + first * sine], axis=-1
    )
    return turned.reshape(values.shape)


def body(
    streams,
    w_query,
    w_key,
    w_value,
    w_output,
    w_gate,
    w_up,
    w_down,
    cache_keys,
    cache_values,
    hc_in,
    hc_res,
    hc_out,
    parents,
    draft_len,
    cache_len,
    accept_pick,
    slot_owner,
):
    highest = lax.Precision.HIGHEST
    local_slots, draft, stream_count, width = streams.shape
    local_width = w_query.shape[1]
    local_heads = local_width // HD
    cache_size = cache_keys.shape[1]
    groups = lax.axis_size("head")
    quarter = draft // groups
    requests = slot_owner.shape[0]
    scale = HD ** (-0.5)
    req_index = lax.axis_index("req")
    everyone = jnp.arange(requests, dtype=jnp.int32)
    my_slots = req_index * local_slots + jnp.arange(local_slots, dtype=jnp.int32)
    slot_pick = everyone[None, :] == my_slots[:, None]
    owner = jnp.sum(jnp.where(slot_pick, slot_owner[None, :], 0), axis=1)
    owner_pick = everyone[None, :] == owner[:, None]

    def lookup(table):
        return jnp.sum(jnp.where(owner_pick, table[None, :], 0), axis=1)

    parent_ids = jnp.sum(jnp.where(owner_pick[:, :, None], parents[None, :, :], 0), axis=1)
    draft_count = lookup(draft_len)
    cache_count = lookup(cache_len)
    accepted = jnp.minimum(lookup(accept_pick), draft_count - 1)
    above, depth = ancestry(parent_ids)
    hidden = streams.astype(jnp.float32)
    mixed_in = jnp.einsum("spmd,m->spd", hidden, hc_in[0], precision=highest)
    normed = normalize(mixed_in).astype(jnp.bfloat16).reshape(local_slots * draft, width)
    position = (cache_count.astype(jnp.float32)[:, None] + depth).reshape(-1)
    query = rotate(
        jnp.dot(normed, w_query, preferred_element_type=jnp.float32), position, HD
    ).astype(jnp.bfloat16)
    keys = rotate(jnp.dot(normed, w_key, preferred_element_type=jnp.float32), position, HD).astype(
        jnp.bfloat16
    )
    values = jnp.dot(normed, w_value, preferred_element_type=jnp.float32).astype(jnp.bfloat16)
    query_h = query.reshape(local_slots, draft, local_heads, HD)
    keys_h = keys.reshape(local_slots, draft, local_heads, HD)
    values_h = values.reshape(local_slots, draft, local_heads, HD)
    stored_keys = cache_keys.reshape(local_slots, cache_size, local_heads, HD)
    stored_values = cache_values.reshape(local_slots, cache_size, local_heads, HD)
    cached = (
        jnp.einsum("sphe,sche->shpc", query_h, stored_keys, preferred_element_type=jnp.float32)
        * scale
    )
    live = jnp.arange(cache_size, dtype=jnp.int32)[None, :] < cache_count[:, None]
    cached = jnp.where(live[:, None, None, :], cached, -1e30)
    local = (
        jnp.einsum("sphe,sqhe->shpq", query_h, keys_h, preferred_element_type=jnp.float32) * scale
    )
    local = jnp.where((above > 0.5)[:, None, :, :], local, -1e30)
    top = jnp.maximum(jnp.max(cached, axis=-1), jnp.max(local, axis=-1))[..., None]
    cached_exp = jnp.exp(cached - top)
    local_exp = jnp.exp(local - top)
    total = jnp.sum(cached_exp, axis=-1, keepdims=True) + jnp.sum(local_exp, axis=-1, keepdims=True)
    weight_cache = (cached_exp / total).astype(jnp.bfloat16)
    weight_local = (local_exp / total).astype(jnp.bfloat16)
    attended = jnp.einsum(
        "shpc,sche->pshe", weight_cache, stored_values, preferred_element_type=jnp.float32
    )
    attended = attended + jnp.einsum(
        "shpq,sqhe->pshe", weight_local, values_h, preferred_element_type=jnp.float32
    )
    attended = attended.astype(jnp.bfloat16).reshape(draft, local_slots, local_width)
    attn_out = lax.psum_scatter(
        jnp.einsum("psk,kd->psd", attended, w_output, preferred_element_type=jnp.float32).astype(
            jnp.bfloat16
        ),
        "head",
        scatter_dimension=0,
        tiled=True,
    ).astype(jnp.float32)
    head_index = lax.axis_index("head")
    first_position = head_index * quarter
    own = lax.dynamic_slice_in_dim(hidden, first_position, quarter, 1)
    carried = jnp.einsum("spnd,nm->spmd", own, hc_res[0], precision=highest)
    carried = (
        carried + hc_out[0][None, None, :, None] * jnp.transpose(attn_out, (1, 0, 2))[:, :, None, :]
    )
    own_rows = local_slots * quarter
    first = carried.astype(jnp.bfloat16).reshape(own_rows, stream_count, width)
    positions_here = first_position + jnp.arange(quarter, dtype=jnp.int32)
    valid = (positions_here[None, :] < draft_count[:, None]).reshape(-1)
    rows_wide = first.astype(jnp.float32)
    normed_rows = normalize(jnp.einsum("nmd,m->nd", rows_wide, hc_in[1], precision=highest)).astype(
        jnp.bfloat16
    )
    piece = lax.all_gather(normed_rows, "req", axis=0, tiled=True)
    gate = jnp.dot(piece, w_gate, preferred_element_type=jnp.float32)
    upward = jnp.dot(piece, w_up, preferred_element_type=jnp.float32)
    inner = (jax.nn.silu(gate) * upward).astype(jnp.bfloat16)
    mlp_out = lax.psum_scatter(
        jnp.dot(inner, w_down, preferred_element_type=jnp.float32).astype(jnp.bfloat16),
        "req",
        scatter_dimension=0,
        tiled=True,
    ).astype(jnp.float32)
    final_rows = jnp.einsum("nkd,km->nmd", rows_wide, hc_res[1], precision=highest)
    final = jnp.where(
        valid[:, None, None], final_rows + hc_out[1][None, :, None] * mlp_out[:, None, :], 0.0
    ).astype(jnp.bfloat16)
    new_streams = final.reshape(local_slots, quarter, stream_count, width)
    nodes = jnp.arange(draft, dtype=jnp.int32)
    path_row = jnp.sum(
        jnp.where((nodes[None, :] == accepted[:, None])[:, :, None], above, 0.0), axis=1
    )
    take = (
        (depth[:, None, :] == nodes.astype(jnp.float32)[None, :, None])
        & (path_row[:, None, :] > 0.5)
    ).astype(jnp.bfloat16)
    keys_rows = keys.reshape(local_slots, draft, local_width)
    values_rows = values.reshape(local_slots, draft, local_width)
    new_keys = jnp.einsum(
        "stq,sqk->stk", take, keys_rows, preferred_element_type=jnp.float32
    ).astype(jnp.bfloat16)
    new_values = jnp.einsum(
        "stq,sqk->stk", take, values_rows, preferred_element_type=jnp.float32
    ).astype(jnp.bfloat16)
    accepted_kv = jnp.stack([new_keys, new_values], axis=2)
    return (new_streams, accepted_kv)


def solution(mesh):
    placed = (
        P("req", None, None, None),
        P(None, "head"),
        P(None, "head"),
        P(None, "head"),
        P("head", None),
        P(None, "req"),
        P(None, "req"),
        P("req", None),
        P("req", None, "head"),
        P("req", None, "head"),
        P(),
        P(),
        P(),
        P(),
        P(),
        P(),
        P(),
        P(),
    )
    return jax.shard_map(
        body,
        mesh=mesh,
        in_specs=placed,
        out_specs=(P("req", "head", None, None), P("req", None, None, "head")),
        check_vma=False,
    )
```

profile of v0, /device:TPU:0, one launch (start us, length us, event | category | flops | bytes accessed | tf_op | source)
XLA Modules:
  0.0 265.1 jit_solution(14680197965514249326)
XLA Ops:
  9.8 0.9 select_reduce_fusion.1
  13.4 8.5 %fusion.58 = f32[1,4,64,2048]{3,0,2,1:T(1,128)S(1)} fusion(bf16[4,64,4,2048]{3,2,1,0:T(4,128)(2,1)} %param.18, f32[2,4]{1,0:T(2,128)S(1)} %copy-done.11), kind=kOutput, calls=%fused_computation.125 | convolution fusion | flops 25165824 | bytes 6291968 | tf_op jit(solution)/shard_map/spmd,m->spd/dot_general | solution.py:86
  26.3 4.0 %copy.77 = bf16[512,2048]{1,0:T(8,128)(2,1)} copy(bf16[512,2048]{0,1:T(8,128)(2,1)} %bitcast.134) | data formatting | bytes 4194304 | tf_op jit(solution)/shard_map/dot_general | solution.py:90
  30.3 1.0 multiply_cosine_fusion
  31.3 2.3 fusion.65
  33.9 4.0 %copy.78 = bf16[512,2048]{1,0:T(8,128)(2,1)} copy(bf16[512,2048]{0,1:T(8,128)(2,1)} %bitcast.135) | data formatting | bytes 4194304 | tf_op jit(solution)/shard_map/dot_general | solution.py:92
  37.9 2.7 %fusion.66 = f32[256,4,128]{0,2,1:T(8,128)S(1)} fusion(bf16[256,2048,1]{1,0,2:T(8,128)(2,1)} %bitcast.142, bf16[4,128,2048]{2,1,0:T(8,128)(2,1)} %bitcast.137), kind=kOutput, calls=%fused_computation.134 | convolution fusion | flops 536870912 | bytes 3670016 | tf_op jit(solution)/shard_map/dot_general | solution.py:92
  41.5 1.2 fusion.64
  42.8 3.8 %fusion.6 = (f32[4,4,64]{2,1,0:T(4,128)S(1)}, f32[4,4,64,1024]{3,2,1,0:T(8,128)S(1)}) fusion(pred[4,1024]{1,0:T(4,128)(4,1)S(1)} %iota_compare_fusion.3, bf16[4,64,4,128]{3,1,0,2:T(8,128)(2,1)S(1)} %bitcast.139, bf16[4,1024,512]{2,1,0:T(8,128)(2,1)} %param.26), kind=kOutput, calls=%fused_computation.10 | convolution fusion | flops 271580160 | bytes 8658944 | tf_op jit(solution)/shard_map/sphe,sche->shpc/dot_general | solution.py:102
  46.7 1.1 fusion.7
  47.8 1.1 copy-done.7
  48.9 1.7 fusion.20
  50.9 1.7 convolution_convert_fusion.1
  52.7 26.1 %reduce-scatter.3.cloned.1.call-done = bf16[16,4,2048]{2,0,1:T(8,128)(2,1)} async-done(((bf16[64,4,2048]{2,0,1:T(8,128)(2,1)}), bf16[16,4,2048]{2,0,1:T(8,128)(2,1)}) %reduce-scatter.3.cloned.1.call-update) | async-done | bytes 262160 | tf_op jit(solution)/shard_map/reduce_scatter | solution.py:124
  78.8 1.0 convert_bitcast_fusion
  79.8 3.4 %fusion.11 = bf16[4,16,4,2048]{3,2,1,0:T(4,128)(2,1)S(1)} fusion(f32[4,16,2048]{2,1,0:T(8,128)S(1)} %convert_bitcast_fusion, f32[4]{0:T(128)S(1)} %get-tuple-element.22, bf16[4,64,4,2048]{3,2,1,0:T(4,128)(2,1)} %param.18, s32[]{:T(128)S(6)} %select_n.38, f32[2,4,4]{2,1,0:T(4,128)S(1)} %copy-done.10), kind=kOutput, calls=%fused_computation.18 | convolution fusion | flops 26738688 | bytes 2624004 | tf_op jit(solution)/shard_map/spnd,nm->spmd/dot_general | solution.py:135
  83.3 1.8 fusion.57
  86.6 52.8 %all-gather.2.cloned.1.call-done = bf16[2048,2048]{1,0:T(8,128)(2,1)} async-done(((bf16[64,2048]{1,0:T(8,128)(2,1)}), bf16[2048,2048]{1,0:T(8,128)(2,1)}) %all-gather.2.cloned.1.call-update) | async-done | bytes 8388624 | tf_op jit(solution)/shard_map/all_gather | solution.py:147
  139.3 7.1 %fusion.67 = f32[2048,256]{1,0:T(8,128)} fusion(bf16[2048,2048]{1,0:T(8,128)(2,1)} %all-gather.2.cloned.1.call-done, bf16[2048,256]{1,0:T(8,128)(2,1)S(1)} %copy-done.9), kind=kOutput, calls=%fused_computation.135 | convolution fusion | flops 2147483648 | bytes 11534336 | tf_op jit(solution)/shard_map/dot_general | solution.py:148
  146.4 13.8 %convolution_convert_fusion = bf16[2048,2048]{1,0:T(8,128)(2,1)} fusion(bf16[256,2048]{1,0:T(8,128)(2,1)} %param.25, bf16[2048,2048]{1,0:T(8,128)(2,1)} %all-gather.2.cloned.1.call-done, bf16[2048,256]{1,0:T(8,128)(2,1)} %param.24, f32[2048,256]{1,0:T(8,128)} %fusion.67), kind=kOutput, calls=%fused_computation | convolution fusion | flops 4302307328 | bytes 20971520 | tf_op jit(solution)/shard_map/dot_general | solution.py:152
  161.7 1.3 copy.69
  163.1 89.6 %reduce-scatter.5.cloned.1.call-done = bf16[64,2048]{1,0:T(8,128)(2,1)} async-done(((bf16[2048,2048]{1,0:T(8,128)(2,1)}), bf16[64,2048]{1,0:T(8,128)(2,1)}) %reduce-scatter.5.cloned.1.call-update) | async-done | bytes 262160 | tf_op jit(solution)/shard_map/reduce_scatter | solution.py:151
  252.7 1.0 convert_element_type.102
  253.7 4.9 %fusion.13 = bf16[64,4,2048]{2,1,0:T(4,128)(2,1)} fusion(bf16[64,4,2048]{2,1,0:T(4,128)(2,1)} %bitcast.146, f32[64,2048]{1,0:T(8,128)S(1)} %convert_element_type.102, f32[4]{0:T(128)S(1)} %get-tuple-element.21, pred[64]{0:T(512)(128)(4,1)S(1)} %lt.43, f32[2,4,4]{2,1,0:T(4,128)S(1)} %copy-done.10), kind=kOutput, calls=%fused_computation.21 | convolution fusion | flops 27262976 | bytes 2624512 | tf_op jit(solution)/shard_map/nkd,km->nmd/dot_general | solution.py:157
  (86 shorter events, 14.3 us)
Async XLA Ops:
  7.2 43.7 %copy-start = (bf16[512,2048]{1,0:T(8,128)(2,1)S(1)}, bf16[512,2048]{1,0:T(8,128)(2,1)}, u32[]{:S(2)}) copy-start(bf16[512,2048]{1,0:T(8,128)(2,1)} %param.22) | copy-start | bytes 6291460
  7.2 6.3 %copy-start.11 = (f32[2,4]{1,0:T(2,128)S(1)}, f32[2,4]{1,0:T(2,128)}, u32[]{:S(2)}) copy-start(f32[2,4]{1,0:T(2,128)} %param.28) | copy-start | bytes 100
  7.2 71.6 %reduce-scatter.3.cloned.1.call-start = ((), (), s32[]{:S(2)}) async-start(), calls=%async_computation.2 | async-start | bytes 1310720 | tf_op jit(solution)/shard_map/reduce_scatter | solution.py:124
  9.6 3.0 %copy-start.5 = (s32[4]{0:T(128)}, s32[4]{0:T(128)S(1)}, u32[]{:S(2)}) copy-start(s32[4]{0:T(128)S(1)} %get-tuple-element.11) | copy-start | bytes 52
  23.2 1.6 copy-start.8
  24.0 7.3 %copy-start.2 = (bf16[4,64,2048]{2,1,0:T(8,128)(2,1)}, bf16[4,64,2048]{2,1,0:T(8,128)(2,1)S(1)}, u32[]{:S(2)}) copy-start(bf16[4,64,2048]{2,1,0:T(8,128)(2,1)S(1)} %multiply_convert_fusion) | copy-start | bytes 3145732
  46.7 2.2 copy-start.7
  48.9 1.7 copy-start.3
  50.9 1.8 copy-start.4
  50.9 28.9 %copy-start.10 = (f32[2,4,4]{2,1,0:T(4,128)S(1)}, f32[2,4,4]{2,1,0:T(4,128)}, u32[]{:S(2)}) copy-start(f32[2,4,4]{2,1,0:T(4,128)} %param.29) | copy-start | bytes 388
  52.6 86.7 %all-gather.2.cloned.1.call-start = ((), (), s32[]{:S(2)}) async-start(), calls=%async_computation.3 | async-start | bytes 8650752 | tf_op jit(solution)/shard_map/all_gather | solution.py:147
  52.7 30.5 %copy-start.12 = (f32[2,4]{1,0:T(2,128)S(1)}, f32[2,4]{1,0:T(2,128)}, u32[]{:S(2)}) copy-start(f32[2,4]{1,0:T(2,128)} %param.28) | copy-start | bytes 100
  83.2 2.4 copy-start.13
  83.2 56.1 %copy-start.9 = (bf16[2048,256]{1,0:T(8,128)(2,1)S(1)}, bf16[2048,256]{1,0:T(8,128)(2,1)}, u32[]{:S(2)}) copy-start(bf16[2048,256]{1,0:T(8,128)(2,1)} %param.23) | copy-start | bytes 3145732
  86.5 166.1 %reduce-scatter.5.cloned.1.call-start = ((), (), s32[]{:S(2)}) async-start(), calls=%async_computation.4 | async-start | bytes 8650752 | tf_op jit(solution)/shard_map/reduce_scatter | solution.py:151
  160.2 0.6 copy-start.6
  253.7 5.0 %copy-start.1 = (bf16[512,2048]{1,0:T(8,128)(2,1)S(1)}, bf16[512,2048]{1,0:T(8,128)(2,1)}, u32[]{:S(2)}) copy-start(bf16[512,2048]{1,0:T(8,128)(2,1)} %param.22) | copy-start | bytes 6291460
Sparse Core Ops, SparseCore 0:
  52.8 26.0 reduce-scatter.2
  86.6 52.6 all-gather.1
  160.4 92.2 reduce-scatter.4
where the time goes:
time: 266 us; the launch traced here: 265 us
  waiting for transfers between devices  169 us (64%)
  matrix products  56.2 us (21%)
  local copies, waits for them, and re-layouts  14.7 us (6%)
  between operations  14.2 us (5%)
  other arithmetic  11.5 us (4%)
    reduce_scatter x1, waiting for transfers between devices, body(): lax.psum_scatter(jnp.dot(inner, w_down, preferred_element_type=jnp.float3...  89.6 us
    all_gather x1, waiting for transfers between devices, body(): piece = lax.all_gather(normed_rows, 'req', axis=0, tiled=True)  52.8 us
    reduce_scatter x1, waiting for transfers between devices, body(): lax.psum_scatter(jnp.einsum('psk,kd->psd', attended, w_output, preferred_...  26.1 us
    dot_general x1, matrix products, body(): jnp.dot(inner, w_down, preferred_element_type=jnp.float32)  13.8 us
    dot_general x1, matrix products, body(): mixed_in = jnp.einsum('spmd,m->spd', hidden, hc_in[0], precision=highest)  8.45 us
    dot_general x1, matrix products, body(): gate = jnp.dot(piece, w_gate, preferred_element_type=jnp.float32)  7.09 us
  transfers between devices with their start and end apart: 3, of which 3 were waited for; matrix products, arithmetic and copies ran while one was open for 1% of the time, Pallas kernels for 0%

commit v1 on v0

--- a/solution.py
+++ b/solution.py
@@ -144,7 +144,9 @@
     normed_rows = normalize(jnp.einsum("nmd,m->nd", rows_wide, hc_in[1], precision=highest)).astype(
         jnp.bfloat16
     )
-    piece = lax.all_gather(normed_rows, "req", axis=0, tiled=True)
+    piece = jnp.concatenate(
+        lax.all_to_all(jnp.stack([normed_rows] * lax.axis_size("req")), "req", 0, 0), axis=0
+    )
     gate = jnp.dot(piece, w_gate, preferred_element_type=jnp.float32)
     upward = jnp.dot(piece, w_up, preferred_element_type=jnp.float32)
     inner = (jax.nn.silu(gate) * upward).astype(jnp.bfloat16)

time: 266 us -> 316 us (1.19)
  blocking collectives: 0 us -> 103 us
  waiting for transfers between devices: 169 us -> 113 us
  local copies, waits for them, and re-layouts: 14.7 us -> 18.9 us
    all_to_all x0 -> x1, blocking collectives: none -> 103 us  [body(): lax.all_to_all(jnp.stack([normed_rows] * lax.axis_size('req')), 'req', 0, 0)]
    all_gather x1 -> x0, waiting for transfers between devices: 52.8 us -> none  [body(): piece = lax.all_gather(normed_rows, 'req', axis=0, tiled=True)]
    dot_general x1, matrix products: 7.09 us -> 3.79 us  [body(): gate = jnp.dot(piece, w_gate, preferred_element_type=jnp.float32)]
    unnamed x29 -> x33, local copies, waits for them, and re-layouts: 3.74 us -> 6.95 us
  transfers between devices with their start and end apart: 3 -> 2, of which waited for: 3 -> 2; matrix products, arithmetic and copies ran while one was open for 1% -> 1% of each run, Pallas kernels for 0% -> 0%
where the time goes in v1:
time: 316 us
  waiting for transfers between devices  113 us (36%)
  blocking collectives  103 us (33%)
  matrix products  56 us (18%)
  local copies, waits for them, and re-layouts  18.9 us (6%)
  between operations  14.5 us (5%)
  other arithmetic  10.8 us (3%)
    all_to_all x1, blocking collectives, body(): lax.all_to_all(jnp.stack([normed_rows] * lax.axis_size('req')), 'req', 0, 0)  103 us
    reduce_scatter x1, waiting for transfers between devices, body(): lax.psum_scatter(jnp.dot(inner, w_down, preferred_element_type=jnp.float3...  86.7 us
    reduce_scatter x1, waiting for transfers between devices, body(): lax.psum_scatter(jnp.einsum('psk,kd->psd', attended, w_output, preferred_...  26.1 us
    dot_general x1, matrix products, body(): jnp.dot(inner, w_down, preferred_element_type=jnp.float32)  16.8 us
    dot_general x1, matrix products, body(): mixed_in = jnp.einsum('spmd,m->spd', hidden, hc_in[0], precision=highest)  8.45 us
    unnamed x33, local copies, waits for them, and re-layouts  6.95 us
  transfers between devices with their start and end apart: 2, of which 2 were waited for; matrix products, arithmetic and copies ran while one was open for 1% of the time, Pallas kernels for 0%

profile of v1, /device:TPU:0, one launch (start us, length us, event | category | flops | bytes accessed | tf_op | source)
XLA Modules:
  0.0 315.6 jit_solution(14907095489104090418)
XLA Ops:
  13.4 8.5 %fusion.58 = f32[1,4,64,2048]{3,0,2,1:T(1,128)S(1)} fusion(bf16[4,64,4,2048]{3,2,1,0:T(4,128)(2,1)} %param.18, f32[2,4]{1,0:T(2,128)S(1)} %copy-done.13), kind=kOutput, calls=%fused_computation.125 | convolution fusion | flops 25165824 | bytes 6291968 | tf_op jit(solution)/shard_map/spmd,m->spd/dot_general | solution.py:86
  26.3 4.0 %copy.77 = bf16[512,2048]{1,0:T(8,128)(2,1)} copy(bf16[512,2048]{0,1:T(8,128)(2,1)} %bitcast.137) | data formatting | bytes 4194304 | tf_op jit(solution)/shard_map/dot_general | solution.py:90
  31.3 2.3 fusion.65
  33.9 4.0 %copy.78 = bf16[512,2048]{1,0:T(8,128)(2,1)} copy(bf16[512,2048]{0,1:T(8,128)(2,1)} %bitcast.138) | data formatting | bytes 4194304 | tf_op jit(solution)/shard_map/dot_general | solution.py:92
  37.9 2.7 fusion.66
  41.5 1.2 fusion.64
  42.8 3.8 %fusion.6 = (f32[4,4,64]{2,1,0:T(4,128)S(1)}, f32[4,4,64,1024]{3,2,1,0:T(8,128)S(1)}) fusion(pred[4,1024]{1,0:T(4,128)(4,1)S(1)} %iota_compare_fusion.3, bf16[4,64,4,128]{3,1,0,2:T(8,128)(2,1)S(1)} %bitcast.142, bf16[4,1024,512]{2,1,0:T(8,128)(2,1)} %param.26), kind=kOutput, calls=%fused_computation.10 | convolution fusion | flops 271580160 | bytes 8658944 | tf_op jit(solution)/shard_map/sphe,sche->shpc/dot_general | solution.py:102
  46.7 1.1 fusion.7
  47.8 1.1 copy-done.8
  48.9 1.7 fusion.20
  50.9 1.7 convolution_convert_fusion.1
  52.7 26.1 %reduce-scatter.3.cloned.1.call-done = bf16[16,4,2048]{2,0,1:T(8,128)(2,1)} async-done(((bf16[64,4,2048]{2,0,1:T(8,128)(2,1)}), bf16[16,4,2048]{2,0,1:T(8,128)(2,1)}) %reduce-scatter.3.cloned.1.call-update) | async-done | bytes 262160 | tf_op jit(solution)/shard_map/reduce_scatter | solution.py:124
  78.8 1.0 convert_bitcast_fusion
  79.8 3.4 %fusion.11 = bf16[4,16,4,2048]{3,2,1,0:T(4,128)(2,1)S(1)} fusion(f32[4,16,2048]{2,1,0:T(8,128)S(1)} %convert_bitcast_fusion, f32[4]{0:T(128)S(1)} %get-tuple-element.22, bf16[4,64,4,2048]{3,2,1,0:T(4,128)(2,1)} %param.18, s32[]{:T(128)S(6)} %select_n.38, f32[2,4,4]{2,1,0:T(4,128)S(1)} %copy-done.12), kind=kOutput, calls=%fused_computation.18 | convolution fusion | flops 26738688 | bytes 2624004 | tf_op jit(solution)/shard_map/spnd,nm->spmd/dot_general | solution.py:135
  83.3 1.8 fusion.57
  85.8 1.1 stack.8
  86.9 102.6 %all_to_all.5 = bf16[32,64,2048]{2,1,0:T(8,128)(2,1)S(1)} all-to-all(bf16[32,64,2048]{2,1,0:T(8,128)(2,1)S(1)} %stack.8), channel_id=1, replica_groups=mesh['req'=32,'head'=4] {'req'}, dimensions={0} | all-to-all | bytes 16777216 | tf_op jit(solution)/shard_map/all_to_all | solution.py:148
  189.4 3.2 %copy-done.2 = bf16[32,64,2048]{2,1,0:T(8,128)(2,1)} copy-done((bf16[32,64,2048]{2,1,0:T(8,128)(2,1)}, bf16[32,64,2048]{2,1,0:T(8,128)(2,1)S(1)}, u32[]{:S(2)}) %copy-start.2) | copy-done | bytes 8388632
  192.6 3.8 %fusion.67 = f32[2048,256]{1,0:T(8,128)} fusion(bf16[2048,2048]{1,0:T(8,128)(2,1)S(1)} %bitcast.135, bf16[2048,256]{1,0:T(8,128)(2,1)S(1)} %copy-done.10), kind=kOutput, calls=%fused_computation.135 | convolution fusion | flops 2147483648 | bytes 11534336 | tf_op jit(solution)/shard_map/dot_general | solution.py:150
  196.4 16.8 %convolution_convert_fusion = bf16[2048,2048]{1,0:T(8,128)(2,1)} fusion(bf16[256,2048]{1,0:T(8,128)(2,1)S(1)} %copy-done.11, bf16[2048,2048]{1,0:T(8,128)(2,1)} %bitcast.136, bf16[2048,256]{1,0:T(8,128)(2,1)} %param.24, f32[2048,256]{1,0:T(8,128)} %fusion.67), kind=kOutput, calls=%fused_computation | convolution fusion | flops 4302307328 | bytes 20971520 | tf_op jit(solution)/shard_map/dot_general | solution.py:154
  214.8 1.3 copy.69
  216.1 86.7 %reduce-scatter.5.cloned.1.call-done = bf16[64,2048]{1,0:T(8,128)(2,1)} async-done(((bf16[2048,2048]{1,0:T(8,128)(2,1)}), bf16[64,2048]{1,0:T(8,128)(2,1)}) %reduce-scatter.5.cloned.1.call-update) | async-done | bytes 262160 | tf_op jit(solution)/shard_map/reduce_scatter | solution.py:153
  302.8 1.0 convert_element_type.102
  303.8 4.9 %fusion.13 = bf16[64,4,2048]{2,1,0:T(4,128)(2,1)} fusion(bf16[64,4,2048]{2,1,0:T(4,128)(2,1)} %bitcast.149, f32[64,2048]{1,0:T(8,128)S(1)} %convert_element_type.102, f32[4]{0:T(128)S(1)} %get-tuple-element.21, pred[64]{0:T(512)(128)(4,1)S(1)} %lt.43, f32[2,4,4]{2,1,0:T(4,128)S(1)} %copy-done.12), kind=kOutput, calls=%fused_computation.21 | convolution fusion | flops 27262976 | bytes 2624512 | tf_op jit(solution)/shard_map/nkd,km->nmd/dot_general | solution.py:159
  (89 shorter events, 15.4 us)
Async XLA Ops:
  7.2 43.7 %copy-start = (bf16[512,2048]{1,0:T(8,128)(2,1)S(1)}, bf16[512,2048]{1,0:T(8,128)(2,1)}, u32[]{:S(2)}) copy-start(bf16[512,2048]{1,0:T(8,128)(2,1)} %param.22) | copy-start | bytes 6291460
  7.2 6.3 %copy-start.13 = (f32[2,4]{1,0:T(2,128)S(1)}, f32[2,4]{1,0:T(2,128)}, u32[]{:S(2)}) copy-start(f32[2,4]{1,0:T(2,128)} %param.28) | copy-start | bytes 100
  7.2 71.6 %reduce-scatter.3.cloned.1.call-start = ((), (), s32[]{:S(2)}) async-start(), calls=%async_computation.3 | async-start | bytes 1310720 | tf_op jit(solution)/shard_map/reduce_scatter | solution.py:124
  9.6 3.0 copy-start.6
  23.2 1.6 copy-start.9
  24.0 7.3 %copy-start.3 = (bf16[4,64,2048]{2,1,0:T(8,128)(2,1)}, bf16[4,64,2048]{2,1,0:T(8,128)(2,1)S(1)}, u32[]{:S(2)}) copy-start(bf16[4,64,2048]{2,1,0:T(8,128)(2,1)S(1)} %multiply_convert_fusion) | copy-start | bytes 3145732
  46.7 2.2 copy-start.8
  48.9 1.7 copy-start.4
  50.9 1.8 copy-start.5
  50.9 28.9 %copy-start.12 = (f32[2,4,4]{2,1,0:T(4,128)S(1)}, f32[2,4,4]{2,1,0:T(4,128)}, u32[]{:S(2)}) copy-start(f32[2,4,4]{2,1,0:T(4,128)} %param.29) | copy-start | bytes 388
  52.6 250.2 %reduce-scatter.5.cloned.1.call-start = ((), (), s32[]{:S(2)}) async-start(), calls=%async_computation.4 | async-start | bytes 8650752 | tf_op jit(solution)/shard_map/reduce_scatter | solution.py:153
  52.7 30.5 %copy-start.14 = (f32[2,4]{1,0:T(2,128)S(1)}, f32[2,4]{1,0:T(2,128)}, u32[]{:S(2)}) copy-start(f32[2,4]{1,0:T(2,128)} %param.28) | copy-start | bytes 100
  83.2 2.3 copy-start.15
  86.9 105.8 %copy-start.10 = (bf16[2048,256]{1,0:T(8,128)(2,1)S(1)}, bf16[2048,256]{1,0:T(8,128)(2,1)}, u32[]{:S(2)}) copy-start(bf16[2048,256]{1,0:T(8,128)(2,1)} %param.23) | copy-start | bytes 3145732
  189.4 3.2 %copy-start.2 = (bf16[32,64,2048]{2,1,0:T(8,128)(2,1)}, bf16[32,64,2048]{2,1,0:T(8,128)(2,1)S(1)}, u32[]{:S(2)}) copy-start(bf16[32,64,2048]{2,1,0:T(8,128)(2,1)S(1)} %all_to_all.5) | copy-start | bytes 25165828
  192.6 3.8 %copy-start.11 = (bf16[256,2048]{1,0:T(8,128)(2,1)S(1)}, bf16[256,2048]{1,0:T(8,128)(2,1)}, u32[]{:S(2)}) copy-start(bf16[256,2048]{1,0:T(8,128)(2,1)} %param.25) | copy-start | bytes 3145732
  213.3 0.6 copy-start.7
  303.8 5.0 %copy-start.1 = (bf16[512,2048]{1,0:T(8,128)(2,1)S(1)}, bf16[512,2048]{1,0:T(8,128)(2,1)}, u32[]{:S(2)}) copy-start(bf16[512,2048]{1,0:T(8,128)(2,1)} %param.22) | copy-start | bytes 6291460
Sparse Core Ops, SparseCore 0:
  52.8 26.0 reduce-scatter.2
  213.4 89.3 reduce-scatter.4
